TPU v7x, 32 devices: a whole 2x2x4 slice. The times are simulated.
32 devices in a mesh: grp: 4 (over y, x), ep: 8 (over z, core).
Axes of the slice: x: 2, y: 2, z: 4, core: 2. Of those that a mesh axis runs over, the one named last changes fastest.
Arguments:
- layer_in: bfloat16 [4096, 1536], P(('grp', 'ep')), may hold values from -6 to 6
- segments: int32 [4096], P(('grp', 'ep')), may hold values from 0 to 4, as said below
- routes: int32 [4096, 8], P(('grp', 'ep')), may hold values from 0 to 23, all different within a row; in each aligned block of 128 rows (0 to 127, 128 to 255, ...) at most 56 rows name the same one
- qkv_weight: bfloat16 [2560, 1536], P('ep'), may hold values from -0.15625 to 0.15625
- out_weight: bfloat16 [1536, 1536], P('ep'), may hold values from -1.25 to 1.25
- router_weight: bfloat16 [24, 1536], P('ep'), may hold values from -0.078125 to 0.078125
- norm1_gain: bfloat16 [1536], P('ep'), may hold values from 0.25 to 1.75
- norm2_gain: bfloat16 [1536], P('ep'), may hold values from 0.25 to 1.75
- w_gate: bfloat16 [24, 512, 1536], P('ep'), may hold values from -0.15625 to 0.15625
- w_up: bfloat16 [24, 512, 1536], P('ep'), may hold values from -0.15625 to 0.15625
- w_down: bfloat16 [24, 512, 1536], P('ep'), may hold values from -1 to 1
- out_cotangent: bfloat16 [4096, 1536], P(('grp', 'ep')), may hold values from -6 to 6
Outputs:
- layer_out: bfloat16 [4096, 1536], P(('grp', 'ep'))
- grad_in: bfloat16 [4096, 1536], P(('grp', 'ep'))
- grad_qkv: float32 [2560, 1536], P('ep')
- grad_out_weight: float32 [1536, 1536], P('ep')
- grad_router: float32 [24, 1536], P('ep')
- grad_norm1: float32 [1536], P('ep')
- grad_norm2: float32 [1536], P('ep')
- grad_gate: float32 [24, 512, 1536], P('ep', None, 'grp')
- grad_up: float32 [24, 512, 1536], P('ep', None, 'grp')
- grad_down: float32 [24, 512, 1536], P('ep', None, 'grp')
Inputs may be any that keep to these rules, and one draw needn't show every extreme that they name: `segments`: within each sequence of 1024 tokens the numbers start at 0 and rise by one at each new document. Every document has at most 800 tokens and each sequence holds one of exactly 800; every document but a sequence's last has 60 or more. `routes`: each row names 8 different experts. In the rows of one device (128 aligned rows) no expert is named by more than 56 rows, a bound that some block reaches.
All inputs are finite; a program needn't handle non-finite values.
Results may differ from a plain program's by a relative error of at most 0.025.
Values may be sent and summed in bfloat16 or wider, within the bound.
No kernel may reach another device: no remote copies, remote signals or barrier semaphores. Data moves between devices by JAX's collectives and lax.ppermute only.
A program may use at most 192 MiB of HBM per device.

v0:
```python
import jax
import jax.numpy as jnp
from jax import lax
from jax.sharding import PartitionSpec as P

QUERY_HEADS = 24
KEY_VALUE_HEADS = 8
HEAD_DIMENSION = 64
TOPK = 8
eps = 1e-06
theta = 10000.0
negative_large = -1e30
f32 = jnp.float32
bf16 = jnp.bfloat16


def angles(token_positions, head_size):
    half = head_size // 2
    freq = theta ** (-jnp.arange(half, dtype=f32) * 2.0 / head_size)
    angle = token_positions.astype(f32)[:, None] * freq[None, :]
    return (jnp.cos(angle)[:, None, :], jnp.sin(angle)[:, None, :])


def rotate(value_matrix, cosine_table, sine_table):
    half = value_matrix.shape[-1] // 2
    first = value_matrix[..., :half]
    second = value_matrix[..., half:]
    return jnp.concatenate(
        [first * cosine_table - second * sine_table, second * cosine_table + first * sine_table],
        axis=-1,
    )


def norm_back(delta, normed, scale, gain):
    scaled = delta * gain
    return scale * (scaled - normed * jnp.mean(scaled * normed, axis=-1, keepdims=True))


def head_plan(devices):
    per_query = QUERY_HEADS // devices
    per_key = KEY_VALUE_HEADS // devices
    blocks = QUERY_HEADS + 2 * KEY_VALUE_HEADS
    own = blocks // devices

    def place(block):
        if block < QUERY_HEADS:
            return (block // per_query, block % per_query)
        block -= QUERY_HEADS
        if block < KEY_VALUE_HEADS:
            return (block // per_key, per_query + block % per_key)
        block -= KEY_VALUE_HEADS
        return (block // per_key, per_query + per_key + block % per_key)

    left = [[(s, *place(i * own + s)) for s in range(own)] for i in range(devices)]
    rounds = []
    for _ in range(own):
        taken = {}

        def assign(i, seen):
            for edge in left[i]:
                j = edge[1]
                if j in seen:
                    continue
                seen.add(j)
                if j not in taken or assign(taken[j][0], seen):
                    taken[j] = (i, edge)
                    return True
            return False

        for i in range(devices):
            assign(i, set())
        source_slot, target, target_slot = ([0] * devices, [0] * devices, [0] * devices)
        for j, (i, edge) in taken.items():
            source_slot[i], target[i], target_slot[j] = (edge[0], j, edge[2])
            left[i].remove(edge)
        rounds.append((source_slot, target, target_slot))
    return rounds


def move_blocks(blocks, pick, pairs, order):
    got = [
        lax.ppermute(lax.dynamic_index_in_dim(blocks, slot, 0, keepdims=False), "ep", pair)
        for slot, pair in zip(pick, pairs)
    ]
    return jnp.stack(got)[order]


def local(
    layer_in,
    segments,
    routes,
    qkv_weight,
    out_weight,
    router_weight,
    norm1_gain,
    norm2_gain,
    w_gate,
    w_up,
    w_down,
    out_cotangent,
):
    tokens, width = layer_in.shape
    devices = lax.axis_size("ep")
    me = lax.axis_index("ep")
    copies = lax.axis_size("grp")
    mine = w_gate.shape[0]
    hidden = w_gate.shape[1]
    experts = mine * devices
    seq = tokens * devices
    capacity = 9 * tokens * TOPK // (8 * mine)
    heads = QUERY_HEADS // devices
    keys = KEY_VALUE_HEADS // devices
    group = heads // keys
    hd = HEAD_DIMENSION
    scale = hd ** (-0.5)
    x_all = lax.all_gather(layer_in, "ep", axis=0, tiled=True)
    gain_width = norm1_gain.shape[0]
    small = jnp.concatenate(
        [
            router_weight.reshape(-1),
            norm1_gain,
            norm2_gain,
            routes.T.astype(bf16).reshape(-1),
            segments.astype(bf16),
        ]
    )
    small_all = lax.all_gather(small, "ep", axis=0, tiled=False)
    cut = mine * width
    full_router = small_all[:, :cut].reshape(experts, width)
    gain_one = small_all[:, cut : cut + gain_width].reshape(1, width).astype(f32)
    gain_two = small_all[:, cut + gain_width : cut + 2 * gain_width].reshape(1, width).astype(f32)
    cut += 2 * gain_width
    routes_all = small_all[:, cut : cut + tokens * TOPK].reshape(devices, TOPK, tokens)
    routes_all = routes_all.transpose(1, 0, 2).reshape(TOPK, seq).astype(jnp.int32)
    seg_all = small_all[:, cut + tokens * TOPK :].reshape(seq)
    rounds = head_plan(devices)
    slots = len(rounds)
    to_heads = [[(i, t[i]) for i in range(devices)] for _, t, _ in rounds]
    to_rows = [[(b, a) for a, b in pair] for pair in to_heads]
    pick_row = [jnp.array(s, jnp.int32)[me] for s, _, _ in rounds]
    pick_head = [jnp.array(s, jnp.int32)[me] for _, _, s in rounds]
    order_head = jnp.array(
        [[[r[2][d] for r in rounds].index(s) for s in range(slots)] for d in range(devices)],
        jnp.int32,
    )[me]
    order_row = jnp.array(
        [[[r[0][d] for r in rounds].index(s) for s in range(slots)] for d in range(devices)],
        jnp.int32,
    )[me]
    block_rows = qkv_weight.shape[0] // slots
    qkv_heads = move_blocks(
        qkv_weight.reshape(slots, block_rows, width), pick_row, to_heads, order_head
    ).reshape(slots * block_rows, width)
    full_out = lax.all_gather(out_weight, "ep", axis=0, tiled=True)
    expert_row = jnp.arange(experts, dtype=jnp.int32)[:, None, None]
    chosen = jnp.any(routes_all[None] == expert_row, axis=1)
    own_chosen = lax.dynamic_slice_in_dim(chosen, me * mine, mine, 0)
    before = (
        jnp.arange(seq, dtype=jnp.int32)[:, None] < jnp.arange(seq, dtype=jnp.int32)[None, :]
    ).astype(bf16)
    rank = jnp.einsum(
        "es,st->et", own_chosen.astype(bf16), before, preferred_element_type=f32
    ).astype(jnp.int32)
    rank = jnp.where(own_chosen, rank, -1)
    places = jnp.arange(capacity, dtype=jnp.int32)[None, :, None]
    pick = rank[:, None, :] == places
    pick_low = pick.astype(bf16).reshape(mine * capacity, seq)
    residual_all = x_all.astype(f32)
    scale_one_all = lax.rsqrt(jnp.mean(residual_all * residual_all, axis=-1, keepdims=True) + eps)
    normed_all = residual_all * scale_one_all
    x_low = (normed_all * gain_one).astype(bf16)
    projected = jnp.einsum("td,cd->tc", x_low, qkv_heads, preferred_element_type=f32)
    positions = jnp.arange(seq, dtype=jnp.int32)
    cosine_table, sine_table = angles(positions, hd)
    turned = rotate(
        projected[:, : (heads + keys) * hd].reshape(seq, heads + keys, hd), cosine_table, sine_table
    ).astype(bf16)
    query = turned[:, :heads].reshape(seq, keys, group, hd).transpose(1, 2, 0, 3)
    key = turned[:, heads:].transpose(1, 0, 2)
    value = (
        projected[:, (heads + keys) * hd :].astype(bf16).reshape(seq, keys, hd).transpose(1, 0, 2)
    )
    valid = (seg_all[:, None] == seg_all[None, :]) & (positions[None, :] <= positions[:, None])
    score = jnp.einsum("hgqd,hkd->hgqk", query, key, preferred_element_type=f32) * scale
    score = jnp.where(valid, score, negative_large)
    top = jnp.max(score, axis=-1, keepdims=True)
    weight = jnp.where(valid, jnp.exp(score - top), 0.0)
    prob = weight / jnp.sum(weight, axis=-1, keepdims=True)
    prob_low = prob.astype(bf16)
    attended = jnp.einsum("hgqk,hkd->hgqd", prob_low, value, preferred_element_type=f32)
    mixed_heads = attended.transpose(2, 0, 1, 3).reshape(seq, heads * hd).astype(bf16)
    mixed = lax.all_to_all(mixed_heads, "ep", split_axis=0, concat_axis=1, tiled=True)
    branch = jnp.einsum("tc,dc->td", mixed, full_out, preferred_element_type=f32)
    hidden_one = layer_in.astype(f32) + branch
    scale_two = lax.rsqrt(jnp.mean(hidden_one * hidden_one, axis=-1, keepdims=True) + eps)
    normed_two = hidden_one * scale_two
    x_two = (normed_two * gain_two).astype(bf16)
    x_two_all = lax.all_gather(x_two, "ep", axis=0, tiled=True)
    late_cotangent, late_mixed, _ = lax.optimization_barrier((out_cotangent, mixed, x_two))
    g_all = lax.all_gather(late_cotangent, "ep", axis=0, tiled=True)
    mixed_all = lax.all_gather(late_mixed, "ep", axis=0, tiled=True)
    logits = jnp.einsum("ed,td->et", full_router, x_two_all, preferred_element_type=f32)
    logits = jnp.where(chosen, logits, negative_large)
    raised = jnp.where(chosen, jnp.exp(logits - jnp.max(logits, axis=0, keepdims=True)), 0.0)
    gates = raised / jnp.sum(raised, axis=0, keepdims=True)
    own_gates = lax.dynamic_slice_in_dim(gates, me * mine, mine, 0)
    place_gate = jnp.sum(jnp.where(pick, own_gates[:, None, :], 0.0), axis=-1)[:, :, None]

    def gather(rows):
        picked = jnp.einsum("pt,td->pd", pick_low, rows, preferred_element_type=f32)
        return picked.astype(bf16).reshape(mine, capacity, width)

    def scatter(rows):
        back = jnp.einsum(
            "pt,pd->td", pick_low, rows.reshape(mine * capacity, width), preferred_element_type=f32
        )
        return back.astype(bf16)

    def shares(left, right):
        grad = jnp.einsum("jcf,jcd->jfd", left, right, preferred_element_type=f32).astype(bf16)
        grad = grad.reshape(mine * hidden, copies, width // copies).transpose(1, 0, 2)
        return grad.reshape(copies * mine * hidden, width // copies)

    def grp_sum(part):
        total = lax.psum_scatter(part, "grp", scatter_dimension=0, tiled=True)
        return total.astype(f32).reshape(mine, hidden, width // copies)

    dense_in = gather(x_two_all)
    dense_g = gather(g_all)
    gate_pre = jnp.einsum("jcd,jfd->jcf", dense_in, w_gate, preferred_element_type=f32)
    up_pre = jnp.einsum("jcd,jfd->jcf", dense_in, w_up, preferred_element_type=f32)
    logistic = jax.nn.sigmoid(gate_pre)
    inner = (gate_pre * logistic * up_pre).astype(bf16)
    expert_out = jnp.einsum("jcf,jfd->jcd", inner, w_down, preferred_element_type=f32)
    place_dgate = jnp.sum(expert_out * dense_g.astype(f32), axis=-1)
    dgate_own = jnp.sum(jnp.where(pick, place_dgate[:, :, None], 0.0), axis=1)
    out_part = scatter((place_gate * expert_out).astype(bf16))
    dense_grad = (place_gate * dense_g.astype(f32)).astype(bf16)
    inner_grad = jnp.einsum("jcd,jfd->jcf", dense_grad, w_down, preferred_element_type=f32)
    gate_back = (inner_grad * up_pre * logistic * (1.0 + gate_pre * (1.0 - logistic))).astype(bf16)
    up_back = (inner_grad * gate_pre * logistic).astype(bf16)
    slot_grad = jnp.einsum(
        "jcf,jfd->jcd", gate_back, w_gate, preferred_element_type=f32
    ) + jnp.einsum("jcf,jfd->jcd", up_back, w_up, preferred_element_type=f32)
    back_part = scatter(slot_grad.astype(bf16))
    two_grad = lax.psum_scatter(back_part, "ep", scatter_dimension=0, tiled=True).astype(f32)
    dgate = lax.all_to_all(dgate_own, "ep", split_axis=1, concat_axis=0, tiled=True)
    down_part = shares(inner, dense_grad)
    gate_part = shares(gate_back, dense_in)
    up_part = shares(up_back, dense_in)
    delta = out_cotangent.astype(f32)
    gates_here = lax.dynamic_slice_in_dim(gates, me * tokens, tokens, 1)
    chosen_grad = gates_here * (dgate - jnp.sum(gates_here * dgate, axis=0, keepdims=True))
    logit_grad = chosen_grad.astype(bf16)
    router_grad = jnp.einsum("et,td->ed", logit_grad, x_two, preferred_element_type=f32)
    two_grad = two_grad + jnp.einsum(
        "et,ed->td", logit_grad, full_router, preferred_element_type=f32
    )
    gain_two_grad = jnp.sum(two_grad * normed_two, axis=0, keepdims=True)
    hidden_grad = delta + norm_back(two_grad, normed_two, scale_two, gain_two)
    hidden_low = hidden_grad.astype(bf16)
    mixing = jnp.einsum("td,dc->tc", hidden_low, full_out, preferred_element_type=f32)
    mixing_heads = lax.all_to_all(
        mixing.astype(bf16), "ep", split_axis=1, concat_axis=0, tiled=True
    )
    hidden_cols = lax.all_to_all(hidden_low, "ep", split_axis=1, concat_axis=0, tiled=True)
    change = mixing_heads.reshape(seq, keys, group, hd).transpose(1, 2, 0, 3)
    prob_grad = jnp.einsum("hgqd,hkd->hgqk", change, value, preferred_element_type=f32)
    row = jnp.sum(prob * prob_grad, axis=-1, keepdims=True)
    score_grad = (prob * (prob_grad - row)).astype(bf16)
    value_grad = jnp.einsum("hgqk,hgqd->hkd", prob_low, change, preferred_element_type=f32)
    query_grad = jnp.einsum("hgqk,hkd->hgqd", score_grad, key, preferred_element_type=f32) * scale
    key_grad = jnp.einsum("hgqk,hgqd->hkd", score_grad, query, preferred_element_type=f32) * scale
    turned_grad = jnp.concatenate(
        [query_grad.transpose(2, 0, 1, 3).reshape(seq, heads, hd), key_grad.transpose(1, 0, 2)],
        axis=1,
    )
    turned_grad = rotate(turned_grad, cosine_table, -sine_table).reshape(seq, (heads + keys) * hd)
    proj_grad = jnp.concatenate(
        [turned_grad, value_grad.transpose(1, 0, 2).reshape(seq, keys * hd)], axis=1
    ).astype(bf16)
    one_part = jnp.einsum("tc,cd->td", proj_grad, qkv_heads, preferred_element_type=f32)
    gain_one_grad = jnp.sum(one_part * normed_all, axis=0, keepdims=True)
    one_grad = lax.psum_scatter(
        one_part.astype(bf16), "ep", scatter_dimension=0, tiled=True
    ).astype(f32)
    qkv_grad = jnp.einsum("tc,td->cd", proj_grad, x_low, preferred_element_type=f32)
    out_grad = jnp.einsum("td,tc->dc", hidden_cols, mixed_all, preferred_element_type=f32)
    small_sum = lax.psum(
        jnp.concatenate([router_grad, gain_one_grad, gain_two_grad], axis=0), ("grp", "ep")
    )
    router_sum = lax.dynamic_slice_in_dim(small_sum[:experts], me * mine, mine, 0)
    gain_sums = lax.dynamic_slice_in_dim(small_sum[experts:], me * gain_width, gain_width, 1)
    qkv_sum = lax.psum(qkv_grad.astype(bf16), "grp")
    qkv_rows = move_blocks(
        qkv_sum.reshape(slots, block_rows, width), pick_head, to_rows, order_row
    ).reshape(slots * block_rows, width)
    out_sum = lax.psum(out_grad.astype(bf16), "grp")
    returned = lax.psum_scatter(out_part, "ep", scatter_dimension=0, tiled=True)
    layer_out = (hidden_one + returned.astype(f32)).astype(bf16)
    residual = layer_in.astype(f32)
    scale_one = lax.rsqrt(jnp.mean(residual * residual, axis=-1, keepdims=True) + eps)
    grad_in = (hidden_grad + norm_back(one_grad, residual * scale_one, scale_one, gain_one)).astype(
        bf16
    )
    return (
        layer_out,
        grad_in,
        qkv_rows.astype(f32),
        out_sum.astype(f32),
        router_sum,
        gain_sums[0],
        gain_sums[1],
        grp_sum(gate_part),
        grp_sum(up_part),
        grp_sum(down_part),
    )


def solution(mesh):
    in_specs = (
        P(("grp", "ep"), None),
        P(("grp", "ep")),
        P(("grp", "ep"), None),
        P("ep", None),
        P("ep", None),
        P("ep", None),
        P("ep"),
        P("ep"),
        P("ep", None, None),
        P("ep", None, None),
        P("ep", None, None),
        P(("grp", "ep"), None),
    )
    out_specs = (
        P(("grp", "ep"), None),
        P(("grp", "ep"), None),
        P("ep", None),
        P("ep", None),
        P("ep", None),
        P("ep"),
        P("ep"),
        P("ep", None, "grp"),
        P("ep", None, "grp"),
        P("ep", None, "grp"),
    )
    return jax.shard_map(local, mesh=mesh, in_specs=in_specs, out_specs=out_specs, check_vma=False)
```

profile of v0, /device:TPU:0, one launch (start us, length us, event | category | flops | bytes accessed | tf_op | source)
XLA Modules:
  0.0 818.6 jit_solution(11952017074831056703)
XLA Ops:
  38.5 27.3 %all-gather = bf16[49152]{0:T(1024)(128)(2,1)S(1)} all-gather(bf16[6144]{0:T(1024)(128)(2,1)S(1)} %concatenate.21), channel_id=2, replica_groups=mesh['grp'=4,'ep'=8] {'ep'}, dimensions={0}, use_global_device_ids=true | all-gather | bytes 110592 | tf_op jit(solution)/shard_map/all_gather | solution.py:127
  80.3 8.1 fusion.87
  88.5 6.1 fusion.29
  100.2 20.0 %all-to-all-done = bf16[8,128,192]{1,2,0:T(8,128)(2,1)S(1)} async-done(((bf16[8,128,192]{1,2,0:T(8,128)(2,1)}), bf16[8,128,192]{1,2,0:T(8,128)(2,1)S(1)}, u32[]{:S(2)}, u32[]{:S(2)}) %all-to-all-start) | async-done | bytes 393248 | tf_op jit(solution)/shard_map/all_to_all | solution.py:192
  131.0 33.4 %all-gather.11.cloned.1.call-done = bf16[1024,1536]{1,0:T(8,128)(2,1)} async-done(((bf16[128,1536]{1,0:T(8,128)(2,1)}), bf16[1024,1536]{1,0:T(8,128)(2,1)}) %all-gather.11.cloned.1.call-update) | async-done | bytes 3145744 | tf_op jit(solution)/shard_map/all_gather | solution.py:198
  168.7 6.2 convolution_convert_fusion.1
  182.3 20.8 %all-gather.13.cloned.1.call-done = bf16[1024,1536]{1,0:T(8,128)(2,1)} async-done(((bf16[128,1536]{1,0:T(8,128)(2,1)}), bf16[1024,1536]{1,0:T(8,128)(2,1)}) %all-gather.13.cloned.1.call-update) | async-done | bytes 3145744 | tf_op jit(solution)/shard_map/all_gather | solution.py:200
  203.1 6.2 convolution_convert_fusion
  209.3 9.0 %fusion.5 = (f32[3,384]{1,0:T(4,128)S(1)}, f32[3,384,1536]{2,1,0:T(8,128)}) fusion(bf16[3,384,1536]{2,1,0:T(8,128)(2,1)S(1)} %bitcast.239, bf16[3,384,512]{2,1,0:T(8,128)(2,1)S(1)} %copy-done.18, bf16[3,512,1536]{2,1,0:T(8,128)(2,1)} %param.34), kind=kOutput, calls=%fused_computation.17 | convolution fusion | flops 1817246592 | bytes 16519680 | tf_op jit(solution)/shard_map/jcf,jfd->jcd/dot_general | solution.py:234
  220.2 6.2 multiply_convert_fusion.3
  231.4 10.6 %bitcast_convert_fusion = bf16[1024,1536]{1,0:T(8,128)(2,1)} fusion(s32[3,1024]{1,0:T(4,128)} %copy-done.30, f32[3,384,1536]{2,1,0:T(8,128)} %fusion.94, bf16[3,384,512]{2,1,0:T(8,128)(2,1)} %get-tuple-element.22, bf16[3,512,1536]{2,1,0:T(8,128)(2,1)} %param.33), kind=kOutput, calls=%fused_computation.23 | convolution fusion | flops 5442109440 | bytes 16134144 | tf_op jit(solution)/shard_map/pt,pd->td/dot_general | solution.py:214
  246.0 5.7 all-to-all-done.1
  255.0 26.7 %reduce-scatter.9.cloned.1.call-done = bf16[128,1536]{1,0:T(8,128)(2,1)} async-done(((bf16[1024,1536]{1,0:T(8,128)(2,1)}), bf16[128,1536]{1,0:T(8,128)(2,1)}) %reduce-scatter.9.cloned.1.call-update) | async-done | bytes 393232 | tf_op jit(solution)/shard_map/reduce_scatter | solution.py:246
  302.7 6.9 all-to-all-done.2
  317.8 6.7 multiply_reduce_fusion
  324.6 8.2 %multiply_convert_fusion = bf16[3,1024,1024]{1,2,0:T(8,128)(2,1)S(1)} fusion(f32[3,1024,1024]{1,2,0:T(8,128)S(1)} %get-tuple-element.58, f32[3,1024]{1,0:T(4,128)S(1)} %get-tuple-element.57, f32[3,1024,1024]{1,2,0:T(8,128)} %get-tuple-element.47, f32[3,1024]{1,0:T(4,128)S(1)} %copy-done.36), kind=kLoop, calls=%fused_computation.3 | loop fusion | flops 12582912 | bytes 31481856 | tf_op jit(solution)/shard_map/convert_element_type | solution.py:270
  352.2 7.2 convolution_convert_fusion.2
  359.4 9.1 %reshape.415 = bf16[1536,4,384]{2,1,0:T(4,128)(2,1)} reshape(bf16[3,512,1536]{2,1,0:T(8,128)(2,1)} %convolution_convert_fusion.2) | data formatting | bytes 9437184 | tf_op jit(solution)/shard_map/reshape | solution.py:221
  373.7 5.7 convolution_convert_fusion.3
  379.4 9.1 %reshape.411 = bf16[1536,4,384]{2,1,0:T(4,128)(2,1)} reshape(bf16[3,512,1536]{2,1,0:T(8,128)(2,1)} %convolution_convert_fusion.3) | data formatting | bytes 9437184 | tf_op jit(solution)/shard_map/reshape | solution.py:221
  388.4 5.1 copy.90
  393.6 5.7 convolution_convert_fusion.4
  399.3 9.1 %reshape.407 = bf16[1536,4,384]{2,1,0:T(4,128)(2,1)} reshape(bf16[3,512,1536]{2,1,0:T(8,128)(2,1)} %convolution_convert_fusion.4) | data formatting | bytes 9437184 | tf_op jit(solution)/shard_map/reshape | solution.py:221
  414.5 9.0 %bitcast_convert_fusion.1 = bf16[1024,1536]{1,0:T(8,128)(2,1)} fusion(f32[3,384,1536]{2,1,0:T(8,128)} %get-tuple-element.53, f32[3,384]{1,0:T(4,128)S(1)} %copy-done.40, s32[3,1024]{1,0:T(4,128)S(1)} %copy-done.32), kind=kOutput, calls=%fused_computation.24 | convolution fusion | flops 3630170112 | bytes 10240512 | tf_op jit(solution)/shard_map/pt,pd->td/dot_general | solution.py:214
  437.7 41.1 %all-reduce.4.cloned.1.call-done = f32[26,1536]{1,0:T(8,128)} async-done(((f32[26,1536]{1,0:T(8,128)}), f32[26,1536]{1,0:T(8,128)}) %all-reduce.4.cloned.1.call-update) | async-done | bytes 159760 | tf_op jit(solution)/shard_map/psum | solution.py:289
  481.2 63.6 %all-reduce.6.cloned.1.call-done = (bf16[5,64,1536]{2,1,0:T(8,128)(2,1)}, bf16[192,1536]{1,0:T(8,128)(2,1)}) async-done(((bf16[5,64,1536]{2,1,0:T(8,128)(2,1)}, bf16[192,1536]{1,0:T(8,128)(2,1)}), (bf16[5,64,1536]{2,1,0:T(8,128)(2,1)}, bf16[192,1536]{1,0:T(8,128)(2,1)})) %all-reduce.6.cloned.1.call-update) | async-done | bytes 1572880 | tf_op jit(solution)/shard_map/psum | solution.py:294
  547.5 6.1 collective-permute-start.9
  564.8 40.0 %reduce-scatter.17.cloned.1.call-done = bf16[1536,384]{1,0:T(8,128)(2,1)} async-done(((bf16[6144,384]{1,0:T(8,128)(2,1)}), bf16[1536,384]{1,0:T(8,128)(2,1)}) %reduce-scatter.17.cloned.1.call-update) | async-done | bytes 1179664 | tf_op jit(solution)/shard_map/reduce_scatter | solution.py:225
  607.6 57.0 %reduce-scatter.15.cloned.1.call-done = bf16[1536,384]{1,0:T(8,128)(2,1)} async-done(((bf16[6144,384]{1,0:T(8,128)(2,1)}), bf16[1536,384]{1,0:T(8,128)(2,1)}) %reduce-scatter.15.cloned.1.call-update) | async-done | bytes 1179664 | tf_op jit(solution)/shard_map/reduce_scatter | solution.py:225
  667.6 57.0 %reduce-scatter.13.cloned.1.call-done = bf16[1536,384]{1,0:T(8,128)(2,1)} async-done(((bf16[6144,384]{1,0:T(8,128)(2,1)}), bf16[1536,384]{1,0:T(8,128)(2,1)}) %reduce-scatter.13.cloned.1.call-update) | async-done | bytes 1179664 | tf_op jit(solution)/shard_map/reduce_scatter | solution.py:225
  727.5 39.7 %reduce-scatter.11.cloned.1.call-done = bf16[128,1536]{1,0:T(8,128)(2,1)} async-done(((bf16[1024,1536]{1,0:T(8,128)(2,1)}), bf16[128,1536]{1,0:T(8,128)(2,1)}) %reduce-scatter.11.cloned.1.call-update) | async-done | bytes 393232 | tf_op jit(solution)/shard_map/reduce_scatter | solution.py:284
  768.5 40.7 %reduce-scatter.7.cloned.1.call-done = bf16[128,1536]{1,0:T(8,128)(2,1)} async-done(((bf16[1024,1536]{1,0:T(8,128)(2,1)}), bf16[128,1536]{1,0:T(8,128)(2,1)}) %reduce-scatter.7.cloned.1.call-update) | async-done | bytes 393232 | tf_op jit(solution)/shard_map/reduce_scatter | solution.py:299
  (293 shorter events, 172.5 us)
Async XLA Ops:
  7.2 65.9 %all-gather.7.cloned.1.call-start = ((), (), s32[]{:S(2)}) async-start(), calls=%async_computation.10 | async-start | bytes 3538944 | tf_op jit(solution)/shard_map/all_gather | solution.py:116
  7.9 113.8 %all-gather.9.cloned.1.call-start = ((), (), s32[]{:S(2)}) async-start(), calls=%async_computation.11 | async-start | bytes 5308416 | tf_op jit(solution)/shard_map/all_gather | solution.py:154
  9.6 62.8 %collective-permute-start.4 = (bf16[64,1536]{1,0:T(8,128)(2,1)}, bf16[64,1536]{1,0:T(8,128)(2,1)S(1)}, u32[]{:S(2)}, u32[]{:S(2)}) collective-permute-start(bf16[64,1536]{1,0:T(8,128)(2,1)} %slice.70), channel_id=1, source_target_pairs={{0,1},{1,3},{2,4},{3,6},{4,0},{5,5},{6,2},{7,7},{8,9},{9,11},{10,1... | collective-permute-start | bytes 589832 | tf_op jit(solution)/shard_map/ppermute | solution.py:82
  26.0 45.4 %collective-permute-start.3 = (bf16[64,1536]{1,0:T(8,128)(2,1)S(1)}, bf16[64,1536]{1,0:T(8,128)(2,1)}, u32[]{:S(2)}, u32[]{:S(2)}) collective-permute-start(bf16[64,1536]{1,0:T(8,128)(2,1)S(1)} %get-tuple-element.33), channel_id=1, source_target_pairs={{0,0},{1,2},{2,3},{3,5},{4,7},{5,4},{6,1},{7,6},{8,8},{9,10},{10,1... | collective-permute-start | bytes 589832 | tf_op jit(solution)/shard_map/ppermute | solution.py:82
  27.4 43.1 %collective-permute-start.2 = (bf16[64,1536]{1,0:T(8,128)(2,1)S(1)}, bf16[64,1536]{1,0:T(8,128)(2,1)}, u32[]{:S(2)}, u32[]{:S(2)}) collective-permute-start(bf16[64,1536]{1,0:T(8,128)(2,1)S(1)} %get-tuple-element.34), channel_id=1, source_target_pairs={{0,1},{1,2},{2,4},{3,6},{4,7},{5,3},{6,0},{7,5},{8,9},{9,10},{10,1... | collective-permute-start | bytes 589832 | tf_op jit(solution)/shard_map/ppermute | solution.py:82
  32.3 37.2 %collective-permute-start.1 = (bf16[64,1536]{1,0:T(8,128)(2,1)S(1)}, bf16[64,1536]{1,0:T(8,128)(2,1)}, u32[]{:S(2)}, u32[]{:S(2)}) collective-permute-start(bf16[64,1536]{1,0:T(8,128)(2,1)S(1)} %get-tuple-element.35), channel_id=1, source_target_pairs={{0,0},{1,1},{2,3},{3,5},{4,6},{5,2},{6,7},{7,4},{8,8},{9,9},{10,11... | collective-permute-start | bytes 589832 | tf_op jit(solution)/shard_map/ppermute | solution.py:82
  33.7 34.8 %collective-permute-start = (bf16[64,1536]{1,0:T(8,128)(2,1)S(1)}, bf16[64,1536]{1,0:T(8,128)(2,1)}, u32[]{:S(2)}, u32[]{:S(2)}) collective-permute-start(bf16[64,1536]{1,0:T(8,128)(2,1)S(1)} %get-tuple-element.36), channel_id=1, source_target_pairs={{0,0},{1,2},{2,4},{3,5},{4,7},{5,1},{6,6},{7,3},{8,8},{9,10},{10,1... | collective-permute-start | bytes 589832 | tf_op jit(solution)/shard_map/ppermute | solution.py:82
  95.4 24.8 %all-to-all-start = ((bf16[8,128,192]{1,2,0:T(8,128)(2,1)}), bf16[8,128,192]{1,2,0:T(8,128)(2,1)S(1)}, u32[]{:S(2)}, u32[]{:S(2)}) async-start(bf16[8,128,192]{1,2,0:T(8,128)(2,1)} %copy.77), calls=%async_computation | async-start | bytes 786432 | tf_op jit(solution)/shard_map/all_to_all | solution.py:192
  100.1 64.3 %all-gather.11.cloned.1.call-start = ((), (), s32[]{:S(2)}) async-start(), calls=%async_computation.12 | async-start | bytes 3538944 | tf_op jit(solution)/shard_map/all_gather | solution.py:198
  127.7 75.4 %all-gather.13.cloned.1.call-start = ((), (), s32[]{:S(2)}) async-start(), calls=%async_computation.14 | async-start | bytes 3538944 | tf_op jit(solution)/shard_map/all_gather | solution.py:200
  128.3 153.4 %reduce-scatter.9.cloned.1.call-start = ((), (), s32[]{:S(2)}) async-start(), calls=%async_computation.15 | async-start | bytes 3538944 | tf_op jit(solution)/shard_map/reduce_scatter | solution.py:246
  242.0 9.6 %all-to-all-start.1 = ((f32[3,8,128]{2,0,1:T(4,128)}), f32[3,8,128]{2,0,1:T(4,128)}, u32[]{:S(2)}, u32[]{:S(2)}) async-start(f32[3,8,128]{2,0,1:T(4,128)} %bitcast.258), calls=%async_computation.3 | async-start | bytes 32768 | tf_op jit(solution)/shard_map/all_to_all | solution.py:247
  293.0 16.6 %all-to-all-start.2 = ((bf16[128,8,192]{0,2,1:T(8,128)(2,1)}), bf16[128,8,192]{0,2,1:T(8,128)(2,1)}, u32[]{:S(2)}, u32[]{:S(2)}) async-start(bf16[128,8,192]{0,2,1:T(8,128)(2,1)} %bitcast.245), calls=%async_computation.4 | async-start | bytes 786432 | tf_op jit(solution)/shard_map/all_to_all | solution.py:263
  297.1 50.8 %all-gather.15.cloned.1.call-start = ((), (), s32[]{:S(2)}) async-start(), calls=%async_computation.17 | async-start | bytes 3538944 | tf_op jit(solution)/shard_map/all_gather | solution.py:201
  309.6 38.3 %all-to-all-start.3 = ((bf16[128,8,192]{0,2,1:T(8,128)(2,1)}), bf16[128,8,192]{0,2,1:T(8,128)(2,1)}, u32[]{:S(2)}, u32[]{:S(2)}) async-start(bf16[128,8,192]{0,2,1:T(8,128)(2,1)} %bitcast.244), calls=%async_computation.6 | async-start | bytes 786432 | tf_op jit(solution)/shard_map/all_to_all | solution.py:266
  313.7 165.1 %all-reduce.4.cloned.1.call-start = ((), (), s32[]{:S(2)}) async-start(), calls=%async_computation.18 | async-start | bytes 393216 | tf_op jit(solution)/shard_map/psum | solution.py:289
  343.4 201.4 %all-reduce.6.cloned.1.call-start = ((), (), s32[]{:S(2)}) async-start(), calls=%async_computation.22 | async-start | bytes 3145728 | tf_op jit(solution)/shard_map/psum | solution.py:294
  351.9 252.9 %reduce-scatter.17.cloned.1.call-start = ((), (), s32[]{:S(2)}) async-start(), calls=%async_computation.21 | async-start | bytes 5898240 | tf_op jit(solution)/shard_map/reduce_scatter | solution.py:225
  373.6 291.0 %reduce-scatter.15.cloned.1.call-start = ((), (), s32[]{:S(2)}) async-start(), calls=%async_computation.20 | async-start | bytes 5898240 | tf_op jit(solution)/shard_map/reduce_scatter | solution.py:225
  393.6 331.0 %reduce-scatter.13.cloned.1.call-start = ((), (), s32[]{:S(2)}) async-start(), calls=%async_computation.19 | async-start | bytes 5898240 | tf_op jit(solution)/shard_map/reduce_scatter | solution.py:225
  413.6 353.6 %reduce-scatter.11.cloned.1.call-start = ((), (), s32[]{:S(2)}) async-start(), calls=%async_computation.16 | async-start | bytes 3538944 | tf_op jit(solution)/shard_map/reduce_scatter | solution.py:284
  414.1 395.1 %reduce-scatter.7.cloned.1.call-start = ((), (), s32[]{:S(2)}) async-start(), calls=%async_computation.13 | async-start | bytes 3538944 | tf_op jit(solution)/shard_map/reduce_scatter | solution.py:299
  546.2 14.6 %collective-permute-start.5 = (bf16[64,1536]{1,0:T(8,128)(2,1)S(1)}, bf16[64,1536]{1,0:T(8,128)(2,1)S(1)}, u32[]{:S(2)}, u32[]{:S(2)}) collective-permute-start(bf16[64,1536]{1,0:T(8,128)(2,1)S(1)} %get-tuple-element.32), channel_id=1, source_target_pairs={{0,0},{2,1},{4,2},{5,3},{7,4},{1,5},{6,6},{3,7},{8,8},{10,9},{12,1... | collective-permute-start | bytes 589832 | tf_op jit(solution)/shard_map/ppermute | solution.py:82
  547.5 15.1 %collective-permute-start.9 = (bf16[64,1536]{1,0:T(8,128)(2,1)S(1)}, bf16[64,1536]{1,0:T(8,128)(2,1)S(1)}, u32[]{:S(2)}, u32[]{:S(2)}) collective-permute-start(bf16[64,1536]{1,0:T(8,128)(2,1)S(1)} %get-tuple-element.28), channel_id=1, source_target_pairs={{1,0},{3,1},{4,2},{6,3},{0,4},{5,5},{2,6},{7,7},{9,8},{11,9},{12,1... | collective-permute-start | bytes 589832 | tf_op jit(solution)/shard_map/ppermute | solution.py:82
  553.6 9.0 %collective-permute-start.8 = (bf16[64,1536]{1,0:T(8,128)(2,1)S(1)}, bf16[64,1536]{1,0:T(8,128)(2,1)S(1)}, u32[]{:S(2)}, u32[]{:S(2)}) collective-permute-start(bf16[64,1536]{1,0:T(8,128)(2,1)S(1)} %get-tuple-element.29), channel_id=1, source_target_pairs={{0,0},{2,1},{3,2},{5,3},{7,4},{4,5},{1,6},{6,7},{8,8},{10,9},{11,1... | collective-permute-start | bytes 589832 | tf_op jit(solution)/shard_map/ppermute | solution.py:82
  554.3 8.3 %collective-permute-start.7 = (bf16[64,1536]{1,0:T(8,128)(2,1)S(1)}, bf16[64,1536]{1,0:T(8,128)(2,1)S(1)}, u32[]{:S(2)}, u32[]{:S(2)}) collective-permute-start(bf16[64,1536]{1,0:T(8,128)(2,1)S(1)} %get-tuple-element.30), channel_id=1, source_target_pairs={{1,0},{2,1},{4,2},{6,3},{7,4},{3,5},{0,6},{5,7},{9,8},{10,9},{12,1... | collective-permute-start | bytes 589832 | tf_op jit(solution)/shard_map/ppermute | solution.py:82
  557.9 2.9 collective-permute-start.6
  664.6 144.6 %copy-start.1 = (f32[128,1536]{1,0:T(8,128)S(1)}, f32[128,1536]{1,0:T(8,128)}, u32[]{:S(2)}) copy-start(f32[128,1536]{1,0:T(8,128)} %copy-done) | copy-start | bytes 2359300
  664.6 144.6 %copy-start.5 = (f32[128,1536]{1,0:T(8,128)S(1)}, f32[128,1536]{1,0:T(8,128)}, u32[]{:S(2)}) copy-start(f32[128,1536]{1,0:T(8,128)} %copy-done.4) | copy-start | bytes 2359300
  664.7 144.6 %copy-start.9 = (bf16[128,1536]{1,0:T(8,128)(2,1)S(1)}, bf16[128,1536]{1,0:T(8,128)(2,1)}, u32[]{:S(2)}) copy-start(bf16[128,1536]{1,0:T(8,128)(2,1)} %param.35) | copy-start | bytes 1179652
  664.7 144.6 %copy-start.38 = (f32[128]{0:T(128)S(1)}, f32[128]{0:T(128)}, u32[]{:S(2)}) copy-start(f32[128]{0:T(128)} %copy-done.37) | copy-start | bytes 1540
  664.7 144.6 %copy-start.44 = (f32[128]{0:T(128)S(1)}, f32[128]{0:T(128)}, u32[]{:S(2)}) copy-start(f32[128]{0:T(128)} %copy-done.43) | copy-start | bytes 1540
  (59 other events, 572.6 us)
Sparse Core Ops, SparseCore 0:
  9.6 49.7 all-gather.6
  61.1 60.6 all-gather.8
  127.8 36.5 all-gather.10
  165.9 37.1 all-gather.12
  242.1 39.5 reduce-scatter.8
  299.2 48.1 all-gather.14
  353.5 125.2 all-reduce.3
  483.1 61.6 all-reduce.5
  547.8 56.9 reduce-scatter.16
  607.7 56.9 reduce-scatter.14
  667.6 56.9 reduce-scatter.12
  726.8 40.3 reduce-scatter.10
  769.5 39.6 reduce-scatter.6
where the time goes:
time: 829 us; the launch traced here: 819 us
  waiting for transfers between devices  458 us (55%)
  matrix products  134 us (16%)
  local copies, waits for them, and re-layouts  83.2 us (10%)
  other arithmetic  41.9 us (5%)
  starting transfers between devices  41.2 us (5%)
  between operations  33 us (4%)
  blocking collectives  27.3 us (3%)
    reduce_scatter x3, waiting for transfers between devices, grp_sum(): total = lax.psum_scatter(part, 'grp', scatter_dimension=0, tiled=True)  154 us
    psum x1, waiting for transfers between devices, local(): qkv_sum = lax.psum(qkv_grad.astype(bf16), 'grp')  63.6 us
    reshape x6, local copies, waits for them, and re-layouts, shares(): grad.reshape(mine * hidden, copies, width // copies).transpose(1, 0, 2)  42.6 us
    psum x1, waiting for transfers between devices, local(): lax.psum(jnp.concatenate([router_grad, gain_one_grad, gain_two_grad], axi...  41.1 us
    reduce_scatter x1, waiting for transfers between devices, local(): returned = lax.psum_scatter(out_part, 'ep', scatter_dimension=0, tiled=True)  40.7 us
    reduce_scatter x1, waiting for transfers between devices, local(): lax.psum_scatter(one_part.astype(bf16), 'ep', scatter_dimension=0, tiled=...  39.7 us
    all_gather x1, waiting for transfers between devices, local(): x_two_all = lax.all_gather(x_two, 'ep', axis=0, tiled=True)  33.4 us
    all_gather x1, blocking collectives, local(): small_all = lax.all_gather(small, 'ep', axis=0, tiled=False)  27.3 us
  transfers between devices with their start and end apart: 27, of which 15 were waited for; matrix products, arithmetic and copies ran while one was open for 24% of the time, Pallas kernels for 0%

commit v1 on v0

--- a/solution.py
+++ b/solution.py
@@ -189,7 +189,10 @@
     prob_low = prob.astype(bf16)
     attended = jnp.einsum("hgqk,hkd->hgqd", prob_low, value, preferred_element_type=f32)
     mixed_heads = attended.transpose(2, 0, 1, 3).reshape(seq, heads * hd).astype(bf16)
-    mixed = lax.all_to_all(mixed_heads, "ep", split_axis=0, concat_axis=1, tiled=True)
+    mixed = jnp.concatenate(
+        lax.all_to_all(jnp.stack(jnp.split(mixed_heads, lax.axis_size("ep"), axis=0)), "ep", 0, 0),
+        axis=1,
+    )
     branch = jnp.einsum("tc,dc->td", mixed, full_out, preferred_element_type=f32)
     hidden_one = layer_in.astype(f32) + branch
     scale_two = lax.rsqrt(jnp.mean(hidden_one * hidden_one, axis=-1, keepdims=True) + eps)

time: 829 us -> 828 us (level)
  transfers between devices with their start and end apart: 27 -> 27, of which waited for: 15 -> 14; matrix products, arithmetic and copies ran while one was open for 24% -> 24% of each run, Pallas kernels for 0% -> 0%
where the time goes in v1:
time: 828 us; the launch traced here: 817 us
  waiting for transfers between devices  453 us (55%)
  matrix products  134 us (16%)
  local copies, waits for them, and re-layouts  87.5 us (11%)
  other arithmetic  42 us (5%)
  starting transfers between devices  41.2 us (5%)
  between operations  33 us (4%)
  blocking collectives  27.2 us (3%)
    reduce_scatter x3, waiting for transfers between devices, grp_sum(): total = lax.psum_scatter(part, 'grp', scatter_dimension=0, tiled=True)  154 us
    psum x1, waiting for transfers between devices, local(): qkv_sum = lax.psum(qkv_grad.astype(bf16), 'grp')  63.6 us
    reshape x6, local copies, waits for them, and re-layouts, shares(): grad.reshape(mine * hidden, copies, width // copies).transpose(1, 0, 2)  42.7 us
    psum x1, waiting for transfers between devices, local(): lax.psum(jnp.concatenate([router_grad, gain_one_grad, gain_two_grad], axi...  40.9 us
    reduce_scatter x1, waiting for transfers between devices, local(): returned = lax.psum_scatter(out_part, 'ep', scatter_dimension=0, tiled=True)  40.7 us
    reduce_scatter x1, waiting for transfers between devices, local(): lax.psum_scatter(one_part.astype(bf16), 'ep', scatter_dimension=0, tiled=...  39.7 us
    all_gather x1, waiting for transfers between devices, local(): x_two_all = lax.all_gather(x_two, 'ep', axis=0, tiled=True)  33.7 us
    all_gather x1, blocking collectives, local(): small_all = lax.all_gather(small, 'ep', axis=0, tiled=False)  27.2 us
  transfers between devices with their start and end apart: 27, of which 14 were waited for; matrix products, arithmetic and copies ran while one was open for 24% of the time, Pallas kernels for 0%

profile of v1, /device:TPU:0, one launch (start us, length us, event | category | flops | bytes accessed | tf_op | source)
XLA Modules:
  0.0 817.3 jit_solution(12486724100422439647)
XLA Ops:
  38.5 27.2 %all-gather = bf16[49152]{0:T(1024)(128)(2,1)S(1)} all-gather(bf16[6144]{0:T(1024)(128)(2,1)S(1)} %concatenate.21), channel_id=2, replica_groups=mesh['grp'=4,'ep'=8] {'ep'}, dimensions={0}, use_global_device_ids=true | all-gather | bytes 110592 | tf_op jit(solution)/shard_map/all_gather | solution.py:127
  80.3 8.0 fusion.91
  88.4 6.1 fusion.32
  104.4 15.8 %all-to-all-done = bf16[8,128,192]{1,2,0:T(8,128)(2,1)S(1)} async-done(((bf16[8,128,192]{1,2,0:T(8,128)(2,1)}), bf16[8,128,192]{1,2,0:T(8,128)(2,1)S(1)}, u32[]{:S(2)}, u32[]{:S(2)}) %all-to-all-start) | async-done | bytes 393248 | tf_op jit(solution)/shard_map/all_to_all | solution.py:193
  129.6 33.7 %all-gather.11.cloned.1.call-done = bf16[1024,1536]{1,0:T(8,128)(2,1)} async-done(((bf16[128,1536]{1,0:T(8,128)(2,1)}), bf16[1024,1536]{1,0:T(8,128)(2,1)}) %all-gather.11.cloned.1.call-update) | async-done | bytes 3145744 | tf_op jit(solution)/shard_map/all_gather | solution.py:201
  167.6 6.2 convolution_convert_fusion.1
  181.1 20.8 %all-gather.13.cloned.1.call-done = bf16[1024,1536]{1,0:T(8,128)(2,1)} async-done(((bf16[128,1536]{1,0:T(8,128)(2,1)}), bf16[1024,1536]{1,0:T(8,128)(2,1)}) %all-gather.13.cloned.1.call-update) | async-done | bytes 3145744 | tf_op jit(solution)/shard_map/all_gather | solution.py:203
  201.9 6.2 convolution_convert_fusion
  208.2 9.0 %fusion.5 = (f32[3,384]{1,0:T(4,128)S(1)}, f32[3,384,1536]{2,1,0:T(8,128)}) fusion(bf16[3,384,1536]{2,1,0:T(8,128)(2,1)S(1)} %bitcast.242, bf16[3,384,512]{2,1,0:T(8,128)(2,1)S(1)} %copy-done.18, bf16[3,512,1536]{2,1,0:T(8,128)(2,1)} %param.34), kind=kOutput, calls=%fused_computation.17 | convolution fusion | flops 1817246592 | bytes 16519680 | tf_op jit(solution)/shard_map/jcf,jfd->jcd/dot_general | solution.py:237
  219.1 6.2 multiply_convert_fusion.3
  230.2 10.6 %bitcast_convert_fusion = bf16[1024,1536]{1,0:T(8,128)(2,1)} fusion(s32[3,1024]{1,0:T(4,128)} %copy-done.30, f32[3,384,1536]{2,1,0:T(8,128)} %fusion.98, bf16[3,384,512]{2,1,0:T(8,128)(2,1)} %get-tuple-element.22, bf16[3,512,1536]{2,1,0:T(8,128)(2,1)} %param.33), kind=kOutput, calls=%fused_computation.23 | convolution fusion | flops 5442109440 | bytes 16134144 | tf_op jit(solution)/shard_map/pt,pd->td/dot_general | solution.py:217
  244.8 5.7 all-to-all-done.1
  253.9 26.7 %reduce-scatter.9.cloned.1.call-done = bf16[128,1536]{1,0:T(8,128)(2,1)} async-done(((bf16[1024,1536]{1,0:T(8,128)(2,1)}), bf16[128,1536]{1,0:T(8,128)(2,1)}) %reduce-scatter.9.cloned.1.call-update) | async-done | bytes 393232 | tf_op jit(solution)/shard_map/reduce_scatter | solution.py:249
  301.6 6.9 all-to-all-done.2
  316.7 6.7 multiply_reduce_fusion
  323.4 8.2 %multiply_convert_fusion = bf16[3,1024,1024]{1,2,0:T(8,128)(2,1)S(1)} fusion(f32[3,1024,1024]{1,2,0:T(8,128)S(1)} %get-tuple-element.66, f32[3,1024]{1,0:T(4,128)S(1)} %get-tuple-element.65, f32[3,1024,1024]{1,2,0:T(8,128)} %get-tuple-element.55, f32[3,1024]{1,0:T(4,128)S(1)} %copy-done.36), kind=kLoop, calls=%fused_computation.3 | loop fusion | flops 12582912 | bytes 31481856 | tf_op jit(solution)/shard_map/convert_element_type | solution.py:273
  351.1 7.2 convolution_convert_fusion.2
  358.3 9.1 %reshape.435 = bf16[1536,4,384]{2,1,0:T(4,128)(2,1)} reshape(bf16[3,512,1536]{2,1,0:T(8,128)(2,1)} %convolution_convert_fusion.2) | data formatting | bytes 9437184 | tf_op jit(solution)/shard_map/reshape | solution.py:224
  372.6 5.7 convolution_convert_fusion.3
  378.3 9.1 %reshape.431 = bf16[1536,4,384]{2,1,0:T(4,128)(2,1)} reshape(bf16[3,512,1536]{2,1,0:T(8,128)(2,1)} %convolution_convert_fusion.3) | data formatting | bytes 9437184 | tf_op jit(solution)/shard_map/reshape | solution.py:224
  392.6 5.7 convolution_convert_fusion.4
  398.3 9.1 %reshape.427 = bf16[1536,4,384]{2,1,0:T(4,128)(2,1)} reshape(bf16[3,512,1536]{2,1,0:T(8,128)(2,1)} %convolution_convert_fusion.4) | data formatting | bytes 9437184 | tf_op jit(solution)/shard_map/reshape | solution.py:224
  407.4 5.1 copy.85
  413.6 9.0 %bitcast_convert_fusion.1 = bf16[1024,1536]{1,0:T(8,128)(2,1)} fusion(f32[3,384,1536]{2,1,0:T(8,128)} %get-tuple-element.61, f32[3,384]{1,0:T(4,128)S(1)} %copy-done.40, s32[3,1024]{1,0:T(4,128)S(1)} %copy-done.32), kind=kOutput, calls=%fused_computation.24 | convolution fusion | flops 3630170112 | bytes 10240512 | tf_op jit(solution)/shard_map/pt,pd->td/dot_general | solution.py:217
  436.7 40.9 %all-reduce.4.cloned.1.call-done = f32[26,1536]{1,0:T(8,128)} async-done(((f32[26,1536]{1,0:T(8,128)}), f32[26,1536]{1,0:T(8,128)}) %all-reduce.4.cloned.1.call-update) | async-done | bytes 159760 | tf_op jit(solution)/shard_map/psum | solution.py:292
  480.0 63.6 %all-reduce.6.cloned.1.call-done = (bf16[5,64,1536]{2,1,0:T(8,128)(2,1)}, bf16[192,1536]{1,0:T(8,128)(2,1)}) async-done(((bf16[5,64,1536]{2,1,0:T(8,128)(2,1)}, bf16[192,1536]{1,0:T(8,128)(2,1)}), (bf16[5,64,1536]{2,1,0:T(8,128)(2,1)}, bf16[192,1536]{1,0:T(8,128)(2,1)})) %all-reduce.6.cloned.1.call-update) | async-done | bytes 1572880 | tf_op jit(solution)/shard_map/psum | solution.py:297
  546.3 6.1 collective-permute-start.9
  563.6 40.0 %reduce-scatter.17.cloned.1.call-done = bf16[1536,384]{1,0:T(8,128)(2,1)} async-done(((bf16[6144,384]{1,0:T(8,128)(2,1)}), bf16[1536,384]{1,0:T(8,128)(2,1)}) %reduce-scatter.17.cloned.1.call-update) | async-done | bytes 1179664 | tf_op jit(solution)/shard_map/reduce_scatter | solution.py:228
  606.5 57.0 %reduce-scatter.15.cloned.1.call-done = bf16[1536,384]{1,0:T(8,128)(2,1)} async-done(((bf16[6144,384]{1,0:T(8,128)(2,1)}), bf16[1536,384]{1,0:T(8,128)(2,1)}) %reduce-scatter.15.cloned.1.call-update) | async-done | bytes 1179664 | tf_op jit(solution)/shard_map/reduce_scatter | solution.py:228
  666.5 57.0 %reduce-scatter.13.cloned.1.call-done = bf16[1536,384]{1,0:T(8,128)(2,1)} async-done(((bf16[6144,384]{1,0:T(8,128)(2,1)}), bf16[1536,384]{1,0:T(8,128)(2,1)}) %reduce-scatter.13.cloned.1.call-update) | async-done | bytes 1179664 | tf_op jit(solution)/shard_map/reduce_scatter | solution.py:228
  726.3 39.7 %reduce-scatter.11.cloned.1.call-done = bf16[128,1536]{1,0:T(8,128)(2,1)} async-done(((bf16[1024,1536]{1,0:T(8,128)(2,1)}), bf16[128,1536]{1,0:T(8,128)(2,1)}) %reduce-scatter.11.cloned.1.call-update) | async-done | bytes 393232 | tf_op jit(solution)/shard_map/reduce_scatter | solution.py:287
  767.3 40.7 %reduce-scatter.7.cloned.1.call-done = bf16[128,1536]{1,0:T(8,128)(2,1)} async-done(((bf16[1024,1536]{1,0:T(8,128)(2,1)}), bf16[128,1536]{1,0:T(8,128)(2,1)}) %reduce-scatter.7.cloned.1.call-update) | async-done | bytes 393232 | tf_op jit(solution)/shard_map/reduce_scatter | solution.py:302
  (300 shorter events, 175.3 us)
Async XLA Ops:
  7.2 65.9 %all-gather.7.cloned.1.call-start = ((), (), s32[]{:S(2)}) async-start(), calls=%async_computation.10 | async-start | bytes 3538944 | tf_op jit(solution)/shard_map/all_gather | solution.py:116
  7.9 112.3 %all-gather.9.cloned.1.call-start = ((), (), s32[]{:S(2)}) async-start(), calls=%async_computation.11 | async-start | bytes 5308416 | tf_op jit(solution)/shard_map/all_gather | solution.py:154
  9.6 62.8 %collective-permute-start.4 = (bf16[64,1536]{1,0:T(8,128)(2,1)}, bf16[64,1536]{1,0:T(8,128)(2,1)S(1)}, u32[]{:S(2)}, u32[]{:S(2)}) collective-permute-start(bf16[64,1536]{1,0:T(8,128)(2,1)} %slice.78), channel_id=1, source_target_pairs={{0,1},{1,3},{2,4},{3,6},{4,0},{5,5},{6,2},{7,7},{8,9},{9,11},{10,1... | collective-permute-start | bytes 589832 | tf_op jit(solution)/shard_map/ppermute | solution.py:82
  26.0 45.4 %collective-permute-start.3 = (bf16[64,1536]{1,0:T(8,128)(2,1)S(1)}, bf16[64,1536]{1,0:T(8,128)(2,1)}, u32[]{:S(2)}, u32[]{:S(2)}) collective-permute-start(bf16[64,1536]{1,0:T(8,128)(2,1)S(1)} %get-tuple-element.33), channel_id=1, source_target_pairs={{0,0},{1,2},{2,3},{3,5},{4,7},{5,4},{6,1},{7,6},{8,8},{9,10},{10,1... | collective-permute-start | bytes 589832 | tf_op jit(solution)/shard_map/ppermute | solution.py:82
  27.4 43.1 %collective-permute-start.2 = (bf16[64,1536]{1,0:T(8,128)(2,1)S(1)}, bf16[64,1536]{1,0:T(8,128)(2,1)}, u32[]{:S(2)}, u32[]{:S(2)}) collective-permute-start(bf16[64,1536]{1,0:T(8,128)(2,1)S(1)} %get-tuple-element.34), channel_id=1, source_target_pairs={{0,1},{1,2},{2,4},{3,6},{4,7},{5,3},{6,0},{7,5},{8,9},{9,10},{10,1... | collective-permute-start | bytes 589832 | tf_op jit(solution)/shard_map/ppermute | solution.py:82
  32.3 37.2 %collective-permute-start.1 = (bf16[64,1536]{1,0:T(8,128)(2,1)S(1)}, bf16[64,1536]{1,0:T(8,128)(2,1)}, u32[]{:S(2)}, u32[]{:S(2)}) collective-permute-start(bf16[64,1536]{1,0:T(8,128)(2,1)S(1)} %get-tuple-element.35), channel_id=1, source_target_pairs={{0,0},{1,1},{2,3},{3,5},{4,6},{5,2},{6,7},{7,4},{8,8},{9,9},{10,11... | collective-permute-start | bytes 589832 | tf_op jit(solution)/shard_map/ppermute | solution.py:82
  33.6 34.9 %collective-permute-start = (bf16[64,1536]{1,0:T(8,128)(2,1)S(1)}, bf16[64,1536]{1,0:T(8,128)(2,1)}, u32[]{:S(2)}, u32[]{:S(2)}) collective-permute-start(bf16[64,1536]{1,0:T(8,128)(2,1)S(1)} %get-tuple-element.36), channel_id=1, source_target_pairs={{0,0},{1,2},{2,4},{3,5},{4,7},{5,1},{6,6},{7,3},{8,8},{9,10},{10,1... | collective-permute-start | bytes 589832 | tf_op jit(solution)/shard_map/ppermute | solution.py:82
  99.6 20.6 %all-to-all-start = ((bf16[8,128,192]{1,2,0:T(8,128)(2,1)}), bf16[8,128,192]{1,2,0:T(8,128)(2,1)S(1)}, u32[]{:S(2)}, u32[]{:S(2)}) async-start(bf16[8,128,192]{1,2,0:T(8,128)(2,1)} %constant_dynamic-update-slice_fusion), calls=%async_computation | async-start | bytes 786432 | tf_op jit(solution)/shard_map/all_to_all | solution.py:193
  104.2 59.0 %all-gather.11.cloned.1.call-start = ((), (), s32[]{:S(2)}) async-start(), calls=%async_computation.12 | async-start | bytes 3538944 | tf_op jit(solution)/shard_map/all_gather | solution.py:201
  126.3 75.7 %all-gather.13.cloned.1.call-start = ((), (), s32[]{:S(2)}) async-start(), calls=%async_computation.14 | async-start | bytes 3538944 | tf_op jit(solution)/shard_map/all_gather | solution.py:203
  126.8 153.7 %reduce-scatter.9.cloned.1.call-start = ((), (), s32[]{:S(2)}) async-start(), calls=%async_computation.15 | async-start | bytes 3538944 | tf_op jit(solution)/shard_map/reduce_scatter | solution.py:249
  240.9 9.6 %all-to-all-start.1 = ((f32[3,8,128]{2,0,1:T(4,128)}), f32[3,8,128]{2,0,1:T(4,128)}, u32[]{:S(2)}, u32[]{:S(2)}) async-start(f32[3,8,128]{2,0,1:T(4,128)} %bitcast.267), calls=%async_computation.3 | async-start | bytes 32768 | tf_op jit(solution)/shard_map/all_to_all | solution.py:250
  291.9 16.6 %all-to-all-start.2 = ((bf16[128,8,192]{0,2,1:T(8,128)(2,1)}), bf16[128,8,192]{0,2,1:T(8,128)(2,1)}, u32[]{:S(2)}, u32[]{:S(2)}) async-start(bf16[128,8,192]{0,2,1:T(8,128)(2,1)} %bitcast.248), calls=%async_computation.4 | async-start | bytes 786432 | tf_op jit(solution)/shard_map/all_to_all | solution.py:266
  296.0 50.8 %all-gather.15.cloned.1.call-start = ((), (), s32[]{:S(2)}) async-start(), calls=%async_computation.17 | async-start | bytes 3538944 | tf_op jit(solution)/shard_map/all_gather | solution.py:204
  308.5 38.3 %all-to-all-start.3 = ((bf16[128,8,192]{0,2,1:T(8,128)(2,1)}), bf16[128,8,192]{0,2,1:T(8,128)(2,1)}, u32[]{:S(2)}, u32[]{:S(2)}) async-start(bf16[128,8,192]{0,2,1:T(8,128)(2,1)} %bitcast.247), calls=%async_computation.6 | async-start | bytes 786432 | tf_op jit(solution)/shard_map/all_to_all | solution.py:269
  312.6 165.1 %all-reduce.4.cloned.1.call-start = ((), (), s32[]{:S(2)}) async-start(), calls=%async_computation.18 | async-start | bytes 393216 | tf_op jit(solution)/shard_map/psum | solution.py:292
  342.3 201.3 %all-reduce.6.cloned.1.call-start = ((), (), s32[]{:S(2)}) async-start(), calls=%async_computation.22 | async-start | bytes 3145728 | tf_op jit(solution)/shard_map/psum | solution.py:297
  350.8 252.8 %reduce-scatter.17.cloned.1.call-start = ((), (), s32[]{:S(2)}) async-start(), calls=%async_computation.21 | async-start | bytes 5898240 | tf_op jit(solution)/shard_map/reduce_scatter | solution.py:228
  372.5 291.0 %reduce-scatter.15.cloned.1.call-start = ((), (), s32[]{:S(2)}) async-start(), calls=%async_computation.20 | async-start | bytes 5898240 | tf_op jit(solution)/shard_map/reduce_scatter | solution.py:228
  392.6 330.9 %reduce-scatter.13.cloned.1.call-start = ((), (), s32[]{:S(2)}) async-start(), calls=%async_computation.19 | async-start | bytes 5898240 | tf_op jit(solution)/shard_map/reduce_scatter | solution.py:228
  412.6 353.4 %reduce-scatter.11.cloned.1.call-start = ((), (), s32[]{:S(2)}) async-start(), calls=%async_computation.16 | async-start | bytes 3538944 | tf_op jit(solution)/shard_map/reduce_scatter | solution.py:287
  413.2 394.8 %reduce-scatter.7.cloned.1.call-start = ((), (), s32[]{:S(2)}) async-start(), calls=%async_computation.13 | async-start | bytes 3538944 | tf_op jit(solution)/shard_map/reduce_scatter | solution.py:302
  545.0 14.6 %collective-permute-start.5 = (bf16[64,1536]{1,0:T(8,128)(2,1)S(1)}, bf16[64,1536]{1,0:T(8,128)(2,1)S(1)}, u32[]{:S(2)}, u32[]{:S(2)}) collective-permute-start(bf16[64,1536]{1,0:T(8,128)(2,1)S(1)} %get-tuple-element.32), channel_id=1, source_target_pairs={{0,0},{2,1},{4,2},{5,3},{7,4},{1,5},{6,6},{3,7},{8,8},{10,9},{12,1... | collective-permute-start | bytes 589832 | tf_op jit(solution)/shard_map/ppermute | solution.py:82
  546.3 15.1 %collective-permute-start.9 = (bf16[64,1536]{1,0:T(8,128)(2,1)S(1)}, bf16[64,1536]{1,0:T(8,128)(2,1)S(1)}, u32[]{:S(2)}, u32[]{:S(2)}) collective-permute-start(bf16[64,1536]{1,0:T(8,128)(2,1)S(1)} %get-tuple-element.28), channel_id=1, source_target_pairs={{1,0},{3,1},{4,2},{6,3},{0,4},{5,5},{2,6},{7,7},{9,8},{11,9},{12,1... | collective-permute-start | bytes 589832 | tf_op jit(solution)/shard_map/ppermute | solution.py:82
  552.4 9.0 %collective-permute-start.8 = (bf16[64,1536]{1,0:T(8,128)(2,1)S(1)}, bf16[64,1536]{1,0:T(8,128)(2,1)S(1)}, u32[]{:S(2)}, u32[]{:S(2)}) collective-permute-start(bf16[64,1536]{1,0:T(8,128)(2,1)S(1)} %get-tuple-element.29), channel_id=1, source_target_pairs={{0,0},{2,1},{3,2},{5,3},{7,4},{4,5},{1,6},{6,7},{8,8},{10,9},{11,1... | collective-permute-start | bytes 589832 | tf_op jit(solution)/shard_map/ppermute | solution.py:82
  553.1 8.3 %collective-permute-start.7 = (bf16[64,1536]{1,0:T(8,128)(2,1)S(1)}, bf16[64,1536]{1,0:T(8,128)(2,1)S(1)}, u32[]{:S(2)}, u32[]{:S(2)}) collective-permute-start(bf16[64,1536]{1,0:T(8,128)(2,1)S(1)} %get-tuple-element.30), channel_id=1, source_target_pairs={{1,0},{2,1},{4,2},{6,3},{7,4},{3,5},{0,6},{5,7},{9,8},{10,9},{12,1... | collective-permute-start | bytes 589832 | tf_op jit(solution)/shard_map/ppermute | solution.py:82
  556.7 2.9 collective-permute-start.6
  663.5 144.5 %copy-start.1 = (f32[128,1536]{1,0:T(8,128)S(1)}, f32[128,1536]{1,0:T(8,128)}, u32[]{:S(2)}) copy-start(f32[128,1536]{1,0:T(8,128)} %copy-done) | copy-start | bytes 2359300
  663.5 144.5 %copy-start.5 = (f32[128,1536]{1,0:T(8,128)S(1)}, f32[128,1536]{1,0:T(8,128)}, u32[]{:S(2)}) copy-start(f32[128,1536]{1,0:T(8,128)} %copy-done.4) | copy-start | bytes 2359300
  663.5 144.5 %copy-start.9 = (bf16[128,1536]{1,0:T(8,128)(2,1)S(1)}, bf16[128,1536]{1,0:T(8,128)(2,1)}, u32[]{:S(2)}) copy-start(bf16[128,1536]{1,0:T(8,128)(2,1)} %param.35) | copy-start | bytes 1179652
  663.5 144.5 %copy-start.38 = (f32[128]{0:T(128)S(1)}, f32[128]{0:T(128)}, u32[]{:S(2)}) copy-start(f32[128]{0:T(128)} %copy-done.37) | copy-start | bytes 1540
  663.5 144.5 %copy-start.44 = (f32[128]{0:T(128)S(1)}, f32[128]{0:T(128)}, u32[]{:S(2)}) copy-start(f32[128]{0:T(128)} %copy-done.43) | copy-start | bytes 1540
  (59 other events, 570.1 us)
Sparse Core Ops, SparseCore 0:
  9.6 49.7 all-gather.6
  61.1 55.6 all-gather.8
  126.4 36.8 all-gather.10
  164.8 37.1 all-gather.12
  241.0 39.5 reduce-scatter.8
  298.0 48.1 all-gather.14
  352.4 125.2 all-reduce.3
  481.9 61.6 all-reduce.5
  546.7 56.9 reduce-scatter.16
  606.5 56.9 reduce-scatter.14
  666.5 56.9 reduce-scatter.12
  725.6 40.3 reduce-scatter.10
  768.3 39.6 reduce-scatter.6
